TPU v7x, 32 devices: a whole 2x2x4 slice. The times are simulated.
32 devices in a mesh: fsdp: 8 (over y, x, core), sp: 4 (over z).
Axes of the slice: x: 2, y: 2, z: 4, core: 2. Of those that a mesh axis runs over, the one named last changes fastest.
Arguments:
- inputs: bfloat16 [32, 1024, 768], P('fsdp', 'sp'), may hold values from -6 to 6
- global_pos: int32 [32, 4], P('fsdp'), may hold values from 0 to 1023, as said below
- w_local: bfloat16 [3, 768, 768], P(None, 'fsdp'), may hold values from -0.21875 to 0.21875
- w_global: bfloat16 [3, 768, 768], P(None, 'fsdp'), may hold values from -0.3125 to 0.3125
- w_out: bfloat16 [768, 768], P('fsdp'), may hold values from -2.5 to 2.5
- b_proj: bfloat16 [6, 768], P(None, 'fsdp'), may hold values from -3 to 3
- gains: bfloat16 [2, 768], P(None, 'fsdp'), may hold values from 0.5 to 1.5
- shifts: bfloat16 [2, 768], P(None, 'fsdp'), may hold values from -3 to 3
- w_in: bfloat16 [768, 3072], P('fsdp'), may hold values from -0.21875 to 0.21875
- c_in: bfloat16 [3072], P('fsdp'), may hold values from -3 to 3
- w_back: bfloat16 [3072, 768], P('fsdp'), may hold values from -0.109375 to 0.109375
- cotangent: bfloat16 [32, 1024, 768], P('fsdp', 'sp'), may hold values from -6 to 6
Outputs:
- output: bfloat16 [32, 1024, 768], P('fsdp', 'sp')
- grad_inputs: bfloat16 [32, 1024, 768], P('fsdp', 'sp')
- grad_w_local: float32 [3, 768, 768], P(None, 'fsdp')
- grad_w_global: float32 [3, 768, 768], P(None, 'fsdp')
- grad_w_out: float32 [768, 768], P('fsdp')
- grad_b_proj: float32 [6, 768], P(None, 'fsdp')
- grad_gains: float32 [2, 768], P(None, 'fsdp')
- grad_shifts: float32 [2, 768], P(None, 'fsdp')
- grad_w_in: float32 [768, 3072], P('fsdp')
- grad_c_in: float32 [3072], P('fsdp')
- grad_w_back: float32 [3072, 768], P('fsdp')
Inputs may be any that keep to these rules, and one draw needn't show every extreme that they name: `global_pos`: in each sequence the 4 global positions are different; the first is 0 and the second is 1023.
All inputs are finite; a program needn't handle non-finite values.
Results may differ from a plain program's by a relative error of at most 0.017.
Values may be sent and summed in bfloat16 or wider, within the bound.
No kernel may reach another device: no remote copies, remote signals or barrier semaphores. Data moves between devices by JAX's collectives and lax.ppermute only.
A program may use at most 256 MiB of HBM per device.

v0:
```python
import jax
import jax.numpy as jnp
from jax import lax
from jax.sharding import PartitionSpec as P

HEADS = 12
HEAD_DIM = 64
WIN = 256
HIGHEST = lax.Precision.HIGHEST
MASKED_SCORE = -1000000000.0
NORM_EPS = 1e-05
BF = jnp.bfloat16
F32 = jnp.float32


def normalize(summed):
    center = summed - jnp.mean(summed, axis=-1, keepdims=True)
    inverse = lax.rsqrt(jnp.mean(center * center, axis=-1, keepdims=True) + NORM_EPS)
    return (center * inverse, inverse)


def norm_back(scaled, normed, inverse):
    return inverse * (
        scaled
        - jnp.mean(scaled, axis=-1, keepdims=True)
        - normed * jnp.mean(scaled * normed, axis=-1, keepdims=True)
    )


def mm(a, b):
    return jnp.dot(a, b, preferred_element_type=F32)


def mm_nt(a, b):
    return lax.dot_general(a, b, (((1,), (1,)), ((), ())), preferred_element_type=F32)


def mm_tn(a, b):
    return lax.dot_general(a, b, (((0,), (0,)), ((), ())), preferred_element_type=F32)


def gelu_pair(inner):
    cdf = 0.5 * (1.0 + lax.erf(inner * 0.5**0.5))
    pdf = jnp.exp(-0.5 * inner * inner) * 0.3989422804014327
    return (inner * cdf, cdf + inner * pdf)


def sequence_step(x, positions, upstream_low, weights):
    w_local, w_global, w_out, b_proj, gains, shifts, w_in, c_in, w_back = weights
    length, width = x.shape
    scale = HEAD_DIM ** (-0.5)
    bias = b_proj.astype(F32)
    gain = gains.astype(F32)
    shift = shifts.astype(F32)

    def heads(value):
        return value.reshape(value.shape[0], HEADS, HEAD_DIM)

    q = heads(((mm(x, w_local[0]) + bias[0]) * scale).astype(BF))
    k = heads(mm(x, w_local[1]).astype(BF))
    v = heads((mm(x, w_local[2]) + bias[1]).astype(BF))
    kg = heads(mm(x, w_global[1]).astype(BF))
    vg = heads((mm(x, w_global[2]) + bias[3]).astype(BF))
    places = jnp.arange(length, dtype=jnp.int32)
    select = positions[:, None] == places[None, :]
    select_low = select.astype(BF)
    select_full = select.astype(F32)
    is_glob = jnp.sum(select_full, axis=0)
    keep_local = 1.0 - is_glob
    rows_glob = mm(select_low, x).astype(BF)
    qg = heads(((mm(rows_glob, w_global[0]) + bias[2]) * scale).astype(BF))
    block = 256
    offsets = list(range(0, length, block))

    def block_scores(offset):
        qb = q[offset : offset + block]
        row_places = offset + jnp.arange(block, dtype=jnp.int32)
        in_band = jnp.abs(row_places[:, None] - places[None, :]) <= WIN
        allowed = in_band | (is_glob[None, :] > 0.5)
        raw = jnp.einsum("ihe,jhe->hij", qb, k, preferred_element_type=F32)
        return (qb, jnp.where(allowed[None], raw, MASKED_SCORE))

    kept = []
    contexts = []
    for offset in offsets:
        qb, masked = block_scores(offset)
        top = jnp.max(masked, axis=-1, keepdims=True)
        powers = jnp.exp(masked - top)
        total = jnp.sum(powers, axis=-1, keepdims=True)
        low = (powers / total).astype(BF)
        contexts.append(jnp.einsum("hij,jhe->ihe", low, v, preferred_element_type=F32))
        kept.append((top, total))
    context_loc = jnp.concatenate(contexts, axis=0)
    glob_scores = jnp.einsum("ghe,jhe->hgj", qg, kg, preferred_element_type=F32)
    glob_probs = jax.nn.softmax(glob_scores, axis=-1)
    glob_low = glob_probs.astype(BF)
    context_glob = jnp.einsum("hgj,jhe->ghe", glob_low, vg, preferred_element_type=F32)
    context = context_loc * keep_local[:, None, None] + jnp.einsum(
        "gl,ghe->lhe", select_full, context_glob, precision=HIGHEST
    )
    merged = context.astype(BF).reshape(length, width)
    attended = mm(merged, w_out) + bias[4]
    normed_one, inverse_one = normalize(x.astype(F32) + attended)
    first_norm = normed_one * gain[0] + shift[0]
    first_low = first_norm.astype(BF)
    inner = mm(first_low, w_in) + c_in.astype(F32)
    act, slope = gelu_pair(inner)
    active = act.astype(BF)
    normed_two, inverse_two = normalize(first_norm + (mm(active, w_back) + bias[5]))
    result = normed_two * gain[1] + shift[1]
    upstream = upstream_low.astype(F32)
    grad_gain_two = jnp.sum(upstream * normed_two, axis=0)
    grad_shift_two = jnp.sum(upstream, axis=0)
    grad_second = norm_back(upstream * gain[1], normed_two, inverse_two)
    branch_grad = grad_second.astype(BF)
    grad_back_w = mm_tn(active, branch_grad)
    grad_out_bias = jnp.sum(branch_grad.astype(F32), axis=0)
    inner_grad = (mm_nt(branch_grad, w_back) * slope).astype(BF)
    grad_in_w = mm_tn(first_low, inner_grad)
    grad_in_bias = jnp.sum(inner_grad.astype(F32), axis=0)
    grad_first = grad_second + mm_nt(inner_grad, w_in)
    grad_gain_one = jnp.sum(grad_first * normed_one, axis=0)
    grad_shift_one = jnp.sum(grad_first, axis=0)
    grad_sum_one = norm_back(grad_first * gain[0], normed_one, inverse_one)
    attn_grad = grad_sum_one.astype(BF)
    grad_out_w = mm_tn(merged, attn_grad)
    grad_att_bias = jnp.sum(attn_grad.astype(F32), axis=0)
    ctx_grad = heads(mm_nt(attn_grad, w_out).astype(BF))
    local_grad = (ctx_grad.astype(F32) * keep_local[:, None, None]).astype(BF)
    glob_ctx_grad = jnp.einsum(
        "gl,lhe->ghe", select_low, ctx_grad, preferred_element_type=F32
    ).astype(BF)
    key_grad = jnp.zeros(k.shape, F32)
    value_grad = jnp.zeros(v.shape, F32)
    query_parts = []
    for index, offset in enumerate(offsets):
        qb, masked = block_scores(offset)
        probs = jnp.exp(masked - kept[index][0]) / kept[index][1]
        low = probs.astype(BF)
        gb = local_grad[offset : offset + block]
        grad_probs = jnp.einsum("ihe,jhe->hij", gb, v, preferred_element_type=F32)
        dot = jnp.sum(probs * grad_probs, axis=-1, keepdims=True)
        score_grad = (probs * (grad_probs - dot)).astype(BF)
        query_parts.append(jnp.einsum("hij,jhe->ihe", score_grad, k, preferred_element_type=F32))
        key_grad = key_grad + jnp.einsum("hij,ihe->jhe", score_grad, qb, preferred_element_type=F32)
        value_grad = value_grad + jnp.einsum("hij,ihe->jhe", low, gb, preferred_element_type=F32)
    dq = jnp.concatenate(query_parts, axis=0).astype(BF)
    glob_grad_probs = jnp.einsum("ghe,jhe->hgj", glob_ctx_grad, vg, preferred_element_type=F32)
    glob_dot = jnp.sum(glob_probs * glob_grad_probs, axis=-1, keepdims=True)
    glob_score_grad = (glob_probs * (glob_grad_probs - glob_dot)).astype(BF)
    dqg = jnp.einsum("hgj,jhe->ghe", glob_score_grad, kg, preferred_element_type=F32).astype(BF)
    dkg = jnp.einsum("hgj,ghe->jhe", glob_score_grad, qg, preferred_element_type=F32).astype(BF)
    dvg = jnp.einsum("hgj,ghe->jhe", glob_low, glob_ctx_grad, preferred_element_type=F32).astype(BF)

    def flat(value):
        return value.astype(BF).reshape(value.shape[0], width)

    dq, dk, dv, dkg, dvg = (flat(value) for value in (dq, key_grad, value_grad, dkg, dvg))
    pre_query = dq * scale
    glob_pre = flat(dqg) * scale
    token_grad = (
        grad_sum_one
        + mm_nt(pre_query, w_local[0])
        + mm_nt(dk, w_local[1])
        + mm_nt(dv, w_local[2])
        + mm_nt(dkg, w_global[1])
        + mm_nt(dvg, w_global[2])
    )
    token_grad = token_grad + jnp.einsum(
        "gr,gd->rd", select_full, mm_nt(glob_pre, w_global[0]), precision=HIGHEST
    )
    grad_local = jnp.stack([mm_tn(x, pre_query), mm_tn(x, dk), mm_tn(x, dv)])
    grad_global = jnp.stack([mm_tn(rows_glob, glob_pre), mm_tn(x, dkg), mm_tn(x, dvg)])

    def total_of(value):
        return jnp.sum(value.astype(F32), axis=0)

    grad_bias = jnp.stack(
        [
            total_of(pre_query),
            total_of(dv),
            total_of(glob_pre),
            total_of(dvg),
            grad_att_bias,
            grad_out_bias,
        ]
    )
    grad_gain = jnp.stack([grad_gain_one, grad_gain_two])
    grad_shift = jnp.stack([grad_shift_one, grad_shift_two])
    return (
        result.astype(BF),
        token_grad.astype(BF),
        (
            grad_local,
            grad_global,
            grad_out_w,
            grad_bias,
            grad_gain,
            grad_shift,
            grad_in_w,
            grad_in_bias,
            grad_back_w,
        ),
    )


def per_device(
    inputs,
    global_pos,
    w_local,
    w_global,
    w_out,
    b_proj,
    gains,
    shifts,
    w_in,
    c_in,
    w_back,
    cotangent,
):
    sp_count = lax.axis_size("sp")
    fsdp_count = lax.axis_size("fsdp")
    sp_index = lax.axis_index("sp")
    own_seqs = inputs.shape[0] // sp_count
    shard = w_out.shape[0]
    width = w_out.shape[1]
    ff_shard = w_back.shape[0]
    pieces = w_in.shape[1] // width

    def to_sequence(value):
        return lax.all_to_all(value, "sp", split_axis=0, concat_axis=1, tiled=True)

    def to_tokens(value):
        return lax.all_to_all(value, "sp", split_axis=1, concat_axis=0, tiled=True)

    x_all = to_sequence(inputs)
    up_all = to_sequence(cotangent)
    own_pos = lax.dynamic_slice_in_dim(global_pos, sp_index * own_seqs, own_seqs, 0)
    small = jnp.concatenate(
        [b_proj.reshape(-1), gains.reshape(-1), shifts.reshape(-1), c_in.reshape(-1)]
    )
    small_rows = -(-small.shape[0] // width)
    small = jnp.pad(small, (0, small_rows * width - small.shape[0])).reshape(small_rows, width)
    pack_one = jnp.concatenate(
        [w_local.reshape(-1, width), w_global.reshape(-1, width), w_out, small], axis=0
    )
    pack_two = jnp.concatenate(
        [w_in.reshape(shard, pieces, width).transpose(1, 0, 2).reshape(-1, width), w_back], axis=0
    )
    all_one = lax.all_gather(pack_one, "fsdp")
    all_two = lax.all_gather(pack_two, "fsdp")

    def part(packed, start):
        return packed[:, start : start + shard].reshape(fsdp_count * shard, width)

    full_local = [part(all_one, index * shard) for index in range(3)]
    full_global = [part(all_one, (3 + index) * shard) for index in range(3)]
    full_out = part(all_one, 6 * shard)
    small_all = all_one[:, 7 * shard :].reshape(fsdp_count, -1)

    def vectors(start, count):
        taken = small_all[:, start : start + count * shard].reshape(fsdp_count, count, shard)
        return taken.transpose(1, 0, 2).reshape(count, fsdp_count * shard)

    full_bias = vectors(0, 6)
    full_gain = vectors(6 * shard, 2)
    full_shift = vectors(8 * shard, 2)
    full_c = small_all[:, 10 * shard : 10 * shard + ff_shard].reshape(-1)
    full_in = jnp.concatenate([part(all_two, index * shard) for index in range(pieces)], axis=1)
    full_back = all_two[:, pieces * shard :].reshape(-1, width)
    weights = (
        full_local,
        full_global,
        full_out,
        full_bias,
        full_gain,
        full_shift,
        full_in,
        full_c,
        full_back,
    )
    results = []
    token_grads = []
    totals = None
    for index in range(own_seqs):
        result, token_grad, grads = sequence_step(
            x_all[index], own_pos[index], up_all[index], weights
        )
        results.append(result)
        token_grads.append(token_grad)
        totals = grads if totals is None else tuple((a + b for a, b in zip(totals, grads)))
    out = to_tokens(jnp.stack(results))
    grad_inputs = to_tokens(jnp.stack(token_grads))
    g_local, g_global, g_out, g_bias, g_gain, g_shift, g_in, g_c, g_back = totals

    def rows(value):
        return value.astype(BF).reshape(-1, fsdp_count, shard, width).transpose(1, 0, 2, 3)

    def cols(value):
        return value.reshape(-1, fsdp_count, shard).transpose(1, 0, 2).reshape(fsdp_count, -1)

    g_small = jnp.concatenate(
        [cols(g_bias), cols(g_gain), cols(g_shift), g_c.reshape(fsdp_count, ff_shard)], axis=1
    ).astype(BF)
    g_small = jnp.pad(g_small, ((0, 0), (0, small_rows * width - g_small.shape[1])))
    first = jnp.concatenate(
        [
            rows(g_in.reshape(width, pieces, width).transpose(1, 0, 2)).reshape(
                fsdp_count, -1, width
            ),
            g_back.astype(BF).reshape(fsdp_count, ff_shard, width),
        ],
        axis=1,
    )
    second = jnp.concatenate(
        [
            rows(g_local).reshape(fsdp_count, -1, width),
            rows(g_global).reshape(fsdp_count, -1, width),
            rows(g_out).reshape(fsdp_count, -1, width),
            g_small.reshape(fsdp_count, small_rows, width),
        ],
        axis=1,
    )

    def reduce(value):
        mine = lax.psum_scatter(value, "fsdp", scatter_dimension=0, tiled=False)
        return lax.psum(mine, "sp").astype(F32)

    first = reduce(first)
    second = reduce(second)
    small_sum = second[7 * shard :].reshape(-1)
    return (
        out,
        grad_inputs,
        second[: 3 * shard].reshape(3, shard, width),
        second[3 * shard : 6 * shard].reshape(3, shard, width),
        second[6 * shard : 7 * shard],
        small_sum[: 6 * shard].reshape(6, shard),
        small_sum[6 * shard : 8 * shard].reshape(2, shard),
        small_sum[8 * shard : 10 * shard].reshape(2, shard),
        first[: pieces * shard]
        .reshape(pieces, shard, width)
        .transpose(1, 0, 2)
        .reshape(shard, pieces * width),
        small_sum[10 * shard : 10 * shard + ff_shard],
        first[pieces * shard :],
    )


def solution(mesh):
    rows = P("fsdp", None)
    tokens = P("fsdp", "sp", None)
    columns = P(None, "fsdp")
    stacked = P(None, "fsdp", None)
    return jax.shard_map(
        per_device,
        mesh=mesh,
        in_specs=(
            tokens,
            rows,
            stacked,
            stacked,
            rows,
            columns,
            columns,
            columns,
            rows,
            P("fsdp"),
            rows,
            tokens,
        ),
        out_specs=(
            tokens,
            tokens,
            stacked,
            stacked,
            rows,
            columns,
            columns,
            columns,
            rows,
            P("fsdp"),
            rows,
        ),
        check_vma=False,
    )
```

profile of v0, /device:TPU:0, one launch (start us, length us, event | category | flops | bytes accessed | tf_op | source)
XLA Modules:
  0.0 702.7 jit_solution(2198869074152670844)
XLA Ops:
  12.7 43.1 %all_to_all.42 = bf16[4,256,768]{2,1,0:T(8,128)(2,1)S(1)} all-to-all(bf16[4,256,768]{2,1,0:T(8,128)(2,1)S(1)} %copy-done.35), channel_id=1, replica_groups=mesh['fsdp'=8,'sp'=4] {'sp'}, dimensions={0} | all-to-all | bytes 3145728 | tf_op jit(solution)/shard_map/all_to_all | solution.py:231
  67.4 28.0 %all-to-all-done.2 = bf16[4,256,768]{2,1,0:T(8,128)(2,1)S(1)} async-done(((bf16[4,256,768]{2,1,0:T(8,128)(2,1)}), bf16[4,256,768]{2,1,0:T(8,128)(2,1)S(1)}, u32[]{:S(2)}, u32[]{:S(2)}) %all-to-all-start.2) | async-done | bytes 1572896 | tf_op jit(solution)/shard_map/all_to_all | solution.py:231
  135.9 11.0 %fusion.132 = (f32[12,256]{1,0:T(8,128)}, f32[12,256,1024]{2,1,0:T(8,128)}) fusion(pred[256,1024]{1,0:T(8,128)(4,1)} %get-tuple-element.82, bf16[256,12,64]{0,2,1:T(8,128)(2,1)} %bitcast.334, bf16[1024,12,64]{0,2,1:T(8,128)(2,1)} %bitcast.255), kind=kOutput, calls=%fused_computation.236 | convolution fusion | flops 412091392 | bytes 14823424 | tf_op jit(solution)/shard_map/sub | solution.py:88
  146.9 10.7 %fusion.133 = (f32[12,256]{1,0:T(8,128)}, f32[12,256,1024]{2,1,0:T(8,128)}) fusion(pred[256,1024]{1,0:T(8,128)(4,1)} %get-tuple-element.81, bf16[256,12,64]{0,2,1:T(8,128)(2,1)} %bitcast.311, bf16[1024,12,64]{0,2,1:T(8,128)(2,1)} %bitcast.256), kind=kOutput, calls=%fused_computation.237 | convolution fusion | flops 412091392 | bytes 14823424 | tf_op jit(solution)/shard_map/sub | solution.py:88
  157.6 10.8 %fusion.134 = (f32[12,256]{1,0:T(8,128)}, f32[12,256,1024]{2,1,0:T(8,128)}) fusion(pred[256,1024]{1,0:T(8,128)(4,1)} %get-tuple-element.80, bf16[256,12,64]{0,2,1:T(8,128)(2,1)} %bitcast.309, bf16[1024,12,64]{0,2,1:T(8,128)(2,1)} %bitcast.257), kind=kOutput, calls=%fused_computation.238 | convolution fusion | flops 412091392 | bytes 14823424 | tf_op jit(solution)/shard_map/sub | solution.py:88
  168.5 11.1 %fusion.135 = (f32[12,256]{1,0:T(8,128)}, f32[12,256,1024]{2,1,0:T(8,128)}) fusion(pred[256,1024]{1,0:T(8,128)(4,1)} %get-tuple-element.79, bf16[256,12,64]{0,2,1:T(8,128)(2,1)S(1)} %bitcast.307, bf16[1024,12,64]{0,2,1:T(8,128)(2,1)} %bitcast.258), kind=kOutput, calls=%fused_computation.239 | convolution fusion | flops 412091392 | bytes 14823424 | tf_op jit(solution)/shard_map/sub | solution.py:88
  217.1 14.2 %multiply_convert_fusion.4 = (bf16[1024,3072]{1,0:T(8,128)(2,1)}, f32[1024,3072]{1,0:T(8,128)}) fusion(f32[3072]{0:T(1024)S(1)} %copy-done.85, bf16[768,768]{1,0:T(8,128)(2,1)} %bitcast.351, bf16[768,768]{1,0:T(8,128)(2,1)} %bitcast.353, bf16[768,768]{1,0:T(8,128)(2,1)} %bitcast.355, bf16[768,768]{1,0:T(8,128)(2,1)} %bitcast.349, ...), kind=kOutput, calls=%fused_computation.20 | convolution fusion | flops 4873519104 | bytes 26765312 | tf_op jit(solution)/shard_map/dot_general | solution.py:31
  231.4 7.7 %fusion.138 = (f32[1024]{0:T(1024)S(1)}, f32[1024,768]{0,1:T(8,128)S(1)}) fusion(f32[768]{0:T(1024)S(1)} %copy-done.96, bf16[1024,3072]{1,0:T(8,128)(2,1)} %get-tuple-element.95, bf16[3072,768]{1,0:T(8,128)(2,1)S(1)} %bitcast.303, f32[768]{0:T(1024)S(1)} %copy-done.94, f32[768]{0:T(1024)S(1)} %mul.222, f32[1024]{0:T(1024)S(1)} %add_rsqrt_fusion.1, ...), kind=kOutput, calls=%fused_computation.242 | convolution fusion | flops 4837342208 | bytes 17323008 | tf_op jit(solution)/shard_map/dot_general | solution.py:31
  244.4 15.1 %fusion.140 = (bf16[3072]{0:T(1024)(128)(2,1)}, bf16[1024,3072]{1,0:T(8,128)(2,1)}) fusion(f32[1024,3072]{1,0:T(8,128)} %get-tuple-element.96, f32[3072]{0:T(1024)S(1)} %copy-done.85, bf16[3072,768]{1,0:T(8,128)(2,1)S(1)} %bitcast.304, f32[1024,768]{0,1:T(8,128)S(1)} %get-tuple-element.52), kind=kOutput, calls=%fused_computation.244 | convolution fusion | flops 4870370304 | bytes 26757120 | tf_op jit(solution)/shard_map/dot_general | solution.py:35
  259.6 9.4 %multiply_reduce_fusion.5 = (bf16[768]{0:T(1024)(128)(2,1)}, f32[1024]{0:T(1024)S(1)}, f32[1024]{0:T(1024)S(1)}, bf16[768]{0:T(1024)(128)(2,1)}, f32[1024,768]{0,1:T(8,128)S(1)}) fusion(f32[1024,768]{0,1:T(8,128)S(1)} %copy-done.14, f32[1024]{0:T(1024)S(1)} %add_rsqrt_fusion.1, f32[1024]{0:T(1024)S(1)} %broadcast_multiply_fusion.4, f32[768]{0:T(1024)S(1)} %mul.222, ...), kind=kOutput, calls=%fused_computation.57 | convolution fusion | flops 4858572800 | bytes 20469760 | tf_op jit(solution)/shard_map/dot_general | solution.py:35
  282.7 8.0 %fusion.41 = f32[12,64,1024]{2,1,0:T(8,128)} fusion(bf16[1024,12,64]{0,2,1:T(8,128)(2,1)S(1)} %multiply_convert_fusion.5, f32[12,256,1024]{2,1,0:T(8,128)} %get-tuple-element.88, f32[12,256]{1,0:T(8,128)S(1)} %copy-done.80), kind=kOutput, calls=%fused_computation.82 | convolution fusion | flops 408944640 | bytes 16138240 | tf_op jit(solution)/shard_map/hij,ihe->jhe/dot_general | solution.py:146
  290.7 8.4 %fusion.37 = f32[12,64,1024]{2,1,0:T(8,128)} fusion(bf16[1024,12,64]{0,2,1:T(8,128)(2,1)S(1)} %multiply_convert_fusion.5, f32[12,256,1024]{2,1,0:T(8,128)} %get-tuple-element.86, f32[12,256]{1,0:T(8,128)S(1)} %copy-done.82), kind=kOutput, calls=%fused_computation.78 | convolution fusion | flops 408944640 | bytes 16138240 | tf_op jit(solution)/shard_map/hij,ihe->jhe/dot_general | solution.py:146
  302.4 8.2 %multiply_reduce_fusion = (f32[12,256]{1,0:T(8,128)}, f32[12,256,1024]{2,1,0:T(8,128)}) fusion(f32[12,256,1024]{2,1,0:T(8,128)S(1)} %bitcast.286, f32[12,256]{1,0:T(8,128)S(1)} %copy-done.78, bf16[1024,12,64]{0,2,1:T(8,128)(2,1)} %bitcast.382, bf16[1024,12,64]{0,2,1:T(8,128)(2,1)S(1)} %multiply_convert_fusion.5), kind=kOutput, calls=%fused_computation.13 | convolution fusion | flops 412087296 | bytes 27160576 | tf_op jit(solution)/shard_map/ihe,jhe->hij/dot_general | solution.py:141
  329.4 7.4 %multiply_reduce_fusion.2 = (f32[12,256]{1,0:T(8,128)S(1)}, f32[12,256,1024]{2,1,0:T(8,128)}) fusion(f32[12,256,1024]{2,1,0:T(8,128)S(1)} %bitcast.290, f32[12,256]{1,0:T(8,128)S(1)} %copy-done.81, bf16[1024,12,64]{0,2,1:T(8,128)(2,1)} %bitcast.384, bf16[1024,12,64]{0,2,1:T(8,128)(2,1)S(1)} %copy-done.40), kind=kOutput, calls=%fused_computation.17 | convolution fusion | flops 412087296 | bytes 27160576 | tf_op jit(solution)/shard_map/ihe,jhe->hij/dot_general | solution.py:141
  348.8 7.6 %multiply_reduce_fusion.3 = (f32[12,256]{1,0:T(8,128)S(1)}, f32[12,256,1024]{2,1,0:T(8,128)}) fusion(f32[12,256,1024]{2,1,0:T(8,128)S(1)} %bitcast.282, f32[12,256]{1,0:T(8,128)S(1)} %copy-done.76, bf16[1024,12,64]{0,2,1:T(8,128)(2,1)} %bitcast.385, bf16[1024,12,64]{0,2,1:T(8,128)(2,1)S(1)} %copy-done.40), kind=kOutput, calls=%fused_computation.19 | convolution fusion | flops 412087296 | bytes 27160576 | tf_op jit(solution)/shard_map/ihe,jhe->hij/dot_general | solution.py:141
  443.7 10.5 %convolution_convert_fusion.1 = bf16[768,3072]{1,0:T(8,128)(2,1)} fusion(bf16[1024,3072]{1,0:T(8,128)(2,1)} %get-tuple-element.117, f32[1024,768]{0,1:T(8,128)S(1)} %copy-done.15, f32[768]{0:T(1024)S(1)} %copy-done.95, f32[768]{0:T(1024)S(1)} %copy-done.72, f32[1024]{0:T(1024)S(1)} %copy-done.74, f32[1024]{0:T(1024)S(1)} %copy-done.67), kind=kOutput, calls=%fused_computation.49 | convolution fusion | flops 4838129664 | bytes 14170112 | tf_op jit(solution)/shard_map/dot_general | solution.py:39
  454.2 9.9 %convert_element_type.322 = bf16[768,4,768]{2,1,0:T(4,128)(2,1)} reshape(bf16[768,3072]{1,0:T(8,128)(2,1)} %convolution_convert_fusion.1) | data formatting | bytes 9437184 | tf_op jit(solution)/shard_map/convert_element_type | solution.py:297
  468.1 8.6 %convolution_convert_fusion = bf16[3072,768]{1,0:T(8,128)(2,1)S(1)} fusion(bf16[1024,3072]{1,0:T(8,128)(2,1)} %get-tuple-element.95, f32[1024,768]{0,1:T(8,128)S(1)} %copy-done.22), kind=kOutput, calls=%fused_computation.48 | convolution fusion | flops 4834983936 | bytes 14155776 | tf_op jit(solution)/shard_map/dot_general | solution.py:39
  481.5 7.6 %copy.94 = bf16[1,1024,768]{2,0,1:T(2,128)(2,1)S(1)} copy(bf16[1,1024,768]{1,2,0:T(8,128)(2,1)} %get-tuple-element.66) | data formatting | bytes 3145728 | tf_op jit(solution)/shard_map/stack | solution.py:292
  489.7 11.8 %reduce.65 = bf16[1024,768]{1,0:T(8,128)(2,1)} reduce(bf16[1024,1,768]{2,1,0:T(2,128)(2,1)S(1)} %bitcast.293, bf16[]{:T(256)} %broadcast.289), dimensions={1}, to_apply=%bitcast.153.reduce_sub_computation | reduce | bytes 3145730
  522.8 7.6 %copy.105 = bf16[1,1024,768]{2,0,1:T(2,128)(2,1)S(1)} copy(bf16[1,1024,768]{1,2,0:T(8,128)(2,1)} %fusion.51) | data formatting | bytes 3145728 | tf_op jit(solution)/shard_map/stack | solution.py:293
  530.4 11.8 %reduce.66 = bf16[1024,768]{1,0:T(8,128)(2,1)} reduce(bf16[1024,1,768]{2,1,0:T(2,128)(2,1)S(1)} %bitcast.294, bf16[]{:T(256)} %broadcast.289), dimensions={1}, to_apply=%bitcast.155.reduce_sub_computation | reduce | bytes 3145730
  551.1 41.6 %reduce-scatter.5.cloned.1.call-done = bf16[1,768,768]{2,1,0:T(8,128)(2,1)} async-done(((bf16[8,768,768]{2,1,0:T(8,128)(2,1)}), bf16[1,768,768]{2,1,0:T(8,128)(2,1)}) %reduce-scatter.5.cloned.1.call-update) | async-done | bytes 1179664 | tf_op jit(solution)/shard_map/reduce_scatter | solution.py:326
  601.7 85.1 %all-reduce.5.cloned.1.call-done = (bf16[674,768]{1,0:T(8,128)(2,1)}, bf16[768,768]{1,0:T(8,128)(2,1)}) async-done(((bf16[674,768]{1,0:T(8,128)(2,1)}, bf16[768,768]{1,0:T(8,128)(2,1)}), (bf16[674,768]{1,0:T(8,128)(2,1)}, bf16[768,768]{1,0:T(8,128)(2,1)})) %all-reduce.5.cloned.1.call-update) | async-done | bytes 2214928 | tf_op jit(solution)/shard_map/psum | solution.py:327
  (450 shorter events, 291.9 us)
Async XLA Ops:
  7.2 55.6 %copy-start = (s32[4,4]{1,0:T(4,128)S(1)}, s32[4,4]{1,0:T(4,128)}, u32[]{:S(2)}) copy-start(s32[4,4]{1,0:T(4,128)} %param.13) | copy-start | bytes 196
  7.2 91.1 %all-gather.8.cloned.1.call-start = ((), (), s32[]{:S(2)}) async-start(), calls=%async_computation.9 | async-start | bytes 9400320 | tf_op jit(solution)/shard_map/all_gather | solution.py:250
  55.8 39.7 %all-to-all-start.2 = ((bf16[4,256,768]{2,1,0:T(8,128)(2,1)}), bf16[4,256,768]{2,1,0:T(8,128)(2,1)S(1)}, u32[]{:S(2)}, u32[]{:S(2)}) async-start(bf16[4,256,768]{2,1,0:T(8,128)(2,1)} %param.23), calls=%async_computation.2 | async-start | bytes 3145728 | tf_op jit(solution)/shard_map/all_to_all | solution.py:231
  59.4 147.3 %all-gather.6.cloned.1.call-start = ((), (), s32[]{:S(2)}) async-start(), calls=%async_computation.8 | async-start | bytes 10616832 | tf_op jit(solution)/shard_map/all_gather | solution.py:251
  62.7 488.4 %reduce-scatter.3.cloned.1.call-start = ((), (), s32[]{:S(2)}) async-start(), calls=%async_computation.6 | async-start | bytes 9400320 | tf_op jit(solution)/shard_map/reduce_scatter | solution.py:326
  62.8 33.0 %copy-start.86 = (s32[4]{0:T(128)}, s32[4]{0:T(128)S(1)}, u32[]{:S(2)}) copy-start(s32[4]{0:T(128)S(1)} %dynamic-slice_bitcast_fusion) | copy-start | bytes 52
  101.0 168.0 %copy-start.71 = (f32[768]{0:T(1024)}, f32[768]{0:T(1024)S(1)}, u32[]{:S(2)}) copy-start(f32[768]{0:T(1024)S(1)} %mul.222) | copy-start | bytes 9220
  129.3 39.1 %copy-start.23 = (bf16[256,768]{0,1:T(8,128)(2,1)}, bf16[256,768]{0,1:T(8,128)(2,1)S(1)}, u32[]{:S(2)}) copy-start(bf16[256,768]{0,1:T(8,128)(2,1)S(1)} %get-tuple-element.67) | copy-start | bytes 1179652
  204.5 64.4 %copy-start.66 = (f32[1024]{0:T(1024)}, f32[1024]{0:T(1024)S(1)}, u32[]{:S(2)}) copy-start(f32[1024]{0:T(1024)S(1)} %broadcast_multiply_fusion.4) | copy-start | bytes 12292
  206.7 62.3 %copy-start.73 = (f32[1024]{0:T(1024)}, f32[1024]{0:T(1024)S(1)}, u32[]{:S(2)}) copy-start(f32[1024]{0:T(1024)S(1)} %add_rsqrt_fusion.1) | copy-start | bytes 12292
  217.1 14.3 %copy-start.96 = (f32[768]{0:T(1024)S(1)}, f32[768]{0:T(1024)}, u32[]{:S(2)}) copy-start(f32[768]{0:T(1024)} %add.238) | copy-start | bytes 9220
  244.4 15.1 %copy-start.21 = (f32[1024,768]{0,1:T(8,128)}, f32[1024,768]{0,1:T(8,128)S(1)}, u32[]{:S(2)}) copy-start(f32[1024,768]{0,1:T(8,128)S(1)} %get-tuple-element.52) | copy-start | bytes 9437188
  244.4 15.1 %copy-start.53 = (bf16[8,96,768]{2,1,0:T(8,128)(2,1)S(1)}, bf16[8,96,768]{2,1,0:T(8,128)(2,1)}, u32[]{:S(2)}) copy-start(bf16[8,96,768]{2,1,0:T(8,128)(2,1)} %get-tuple-element.55) | copy-start | bytes 3538948
  244.4 15.1 %copy-start.54 = (bf16[8,96,768]{2,1,0:T(8,128)(2,1)S(1)}, bf16[8,96,768]{2,1,0:T(8,128)(2,1)}, u32[]{:S(2)}) copy-start(bf16[8,96,768]{2,1,0:T(8,128)(2,1)} %get-tuple-element.56) | copy-start | bytes 3538948
  244.4 15.1 %copy-start.55 = (bf16[8,96,768]{2,1,0:T(8,128)(2,1)S(1)}, bf16[8,96,768]{2,1,0:T(8,128)(2,1)}, u32[]{:S(2)}) copy-start(bf16[8,96,768]{2,1,0:T(8,128)(2,1)} %get-tuple-element.57) | copy-start | bytes 3538948
  244.4 15.1 %copy-start.56 = (bf16[8,96,768]{2,1,0:T(8,128)(2,1)S(1)}, bf16[8,96,768]{2,1,0:T(8,128)(2,1)}, u32[]{:S(2)}) copy-start(bf16[8,96,768]{2,1,0:T(8,128)(2,1)} %get-tuple-element.58) | copy-start | bytes 3538948
  275.8 34.8 %copy-start.39 = (bf16[1024,12,64]{0,2,1:T(8,128)(2,1)}, bf16[1024,12,64]{0,2,1:T(8,128)(2,1)S(1)}, u32[]{:S(2)}) copy-start(bf16[1024,12,64]{0,2,1:T(8,128)(2,1)S(1)} %multiply_convert_fusion.5) | copy-start | bytes 4718596
  282.7 16.4 %slice-start.9 = ((s8[12582912]{0:T(1024)(128)(4,1)}), s8[4194304]{0:T(1024)(128)(4,1)S(1)}, s32[]{:S(2)}) async-start(s8[12582912]{0:T(1024)(128)(4,1)} %bitcast.285), calls=%async_computation.20 | async-start | bytes 8388608
  282.7 16.4 %slice-start.10 = ((s8[12582912]{0:T(1024)(128)(4,1)}), s8[4194304]{0:T(1024)(128)(4,1)S(1)}, s32[]{:S(2)}) async-start(s8[12582912]{0:T(1024)(128)(4,1)} %bitcast.285), calls=%async_computation.21 | async-start | bytes 8388608
  344.8 33.2 %copy-start.27 = (bf16[12,64,256]{2,1,0:T(8,128)(2,1)}, bf16[12,64,256]{2,1,0:T(8,128)(2,1)S(1)}, u32[]{:S(2)}) copy-start(bf16[12,64,256]{2,1,0:T(8,128)(2,1)S(1)} %convolution_convert_fusion.16) | copy-start | bytes 1179652
  441.9 150.9 %reduce-scatter.5.cloned.1.call-start = ((), (), s32[]{:S(2)}) async-start(), calls=%async_computation.7 | async-start | bytes 10616832 | tf_op jit(solution)/shard_map/reduce_scatter | solution.py:326
  505.3 40.7 %all-to-all-start.1 = ((bf16[4,2,98304]{2,1,0:T(2,128)(2,1)}), bf16[4,2,98304]{2,1,0:T(2,128)(2,1)}, u32[]{:S(2)}, u32[]{:S(2)}) async-start(bf16[4,2,98304]{2,1,0:T(2,128)(2,1)} %reshape.661), calls=%async_computation.1 | async-start | bytes 3145728 | tf_op jit(solution)/shard_map/all_to_all | solution.py:234
  546.0 51.2 %all-to-all-start.3 = ((bf16[4,2,98304]{2,1,0:T(2,128)(2,1)}), bf16[4,2,98304]{2,1,0:T(2,128)(2,1)}, u32[]{:S(2)}, u32[]{:S(2)}) async-start(bf16[4,2,98304]{2,1,0:T(2,128)(2,1)} %reshape.663), calls=%async_computation.3 | async-start | bytes 3145728 | tf_op jit(solution)/shard_map/all_to_all | solution.py:234
  551.1 135.7 %all-reduce.5.cloned.1.call-start = ((), (), s32[]{:S(2)}) async-start(), calls=%async_computation.10 | async-start | bytes 4448256 | tf_op jit(solution)/shard_map/psum | solution.py:327
  (112 other events, 473.0 us)
Sparse Core Ops, SparseCore 0:
  12.8 56.9 all-gather.7
  72.3 58.8 all-gather.5
  442.0 70.4 reduce-scatter.2
  516.2 76.4 reduce-scatter.4
  595.2 91.5 all-reduce.4
where the time goes:
time: 709 us; the launch traced here: 703 us
  matrix products  269 us (38%)
  waiting for transfers between devices  155 us (22%)
  local copies, waits for them, and re-layouts  129 us (18%)
  other arithmetic  77.2 us (11%)
  blocking collectives  43.1 us (6%)
  between operations  15.4 us (2%)
  starting transfers between devices  13.4 us (2%)
    psum x1, waiting for transfers between devices, reduce(): return lax.psum(mine, 'sp').astype(F32)  85.1 us
    sub x4, matrix products, sequence_step(): powers = jnp.exp(masked - top)  43.7 us
    all_to_all x1, blocking collectives, to_sequence(): return lax.all_to_all(value, 'sp', split_axis=0, concat_axis=1, tiled=True)  43.1 us
    unnamed x271, local copies, waits for them, and re-layouts  42.3 us
    reduce_scatter x2, waiting for transfers between devices, reduce(): mine = lax.psum_scatter(value, 'fsdp', scatter_dimension=0, tiled=False)  41.6 us
    dot_general x9, matrix products, mm_tn(): lax.dot_general(a, b, (((0,), (0,)), ((), ())), preferred_element_type=F32)  38.9 us
    dot_general x10, matrix products, mm(): return jnp.dot(a, b, preferred_element_type=F32)  38.8 us
    dot_general x9, matrix products, mm_nt(): lax.dot_general(a, b, (((1,), (1,)), ((), ())), preferred_element_type=F32)  33.3 us
  transfers between devices with their start and end apart: 8, of which 3 were waited for; matrix products, arithmetic and copies ran while one was open for 31% of the time, Pallas kernels for 0%

commit v1 on v0

--- a/solution.py
+++ b/solution.py
@@ -324,7 +324,7 @@
 
     def reduce(value):
         mine = lax.psum_scatter(value, "fsdp", scatter_dimension=0, tiled=False)
-        return lax.psum(mine, "sp").astype(F32)
+        return jnp.sum(lax.all_gather(mine, "sp"), axis=0).astype(F32)
 
     first = reduce(first)
     second = reduce(second)

time: 709 us -> 838 us (1.18)
  waiting for transfers between devices: 155 us -> 280 us
    all_to_all x2, waiting for transfers between devices: 0.01 us -> 112 us  [to_tokens(): return lax.all_to_all(value, 'sp', split_axis=1, concat_axis=0, tiled=True)]
    psum x1 -> x0, waiting for transfers between devices: 85.1 us -> none  [reduce(): return lax.psum(mine, 'sp').astype(F32)]
    reduce_scatter x2, waiting for transfers between devices: 41.6 us -> 112 us  [reduce(): mine = lax.psum_scatter(value, 'fsdp', scatter_dimension=0, tiled=False)]
    all_gather x0 -> x2, waiting for transfers between devices: none -> 28.6 us  [reduce(): return jnp.sum(lax.all_gather(mine, 'sp'), axis=0).astype(F32)]
    unnamed x271 -> x269, local copies, waits for them, and re-layouts: 42.3 us -> 41.3 us
  transfers between devices with their start and end apart: 8 -> 9, of which waited for: 3 -> 6; matrix products, arithmetic and copies ran while one was open for 31% -> 27% of each run, Pallas kernels for 0% -> 0%
where the time goes in v1:
time: 838 us; the launch traced here: 832 us
  waiting for transfers between devices  280 us (33%)
  matrix products  269 us (32%)
  local copies, waits for them, and re-layouts  125 us (15%)
  other arithmetic  84.6 us (10%)
  blocking collectives  43.1 us (5%)
  between operations  16 us (2%)
  starting transfers between devices  13.3 us (2%)
    all_to_all x2, waiting for transfers between devices, to_tokens(): return lax.all_to_all(value, 'sp', split_axis=1, concat_axis=0, tiled=True)  112 us
    reduce_scatter x2, waiting for transfers between devices, reduce(): mine = lax.psum_scatter(value, 'fsdp', scatter_dimension=0, tiled=False)  112 us
    sub x4, matrix products, sequence_step(): powers = jnp.exp(masked - top)  43.6 us
    all_to_all x1, blocking collectives, to_sequence(): return lax.all_to_all(value, 'sp', split_axis=0, concat_axis=1, tiled=True)  43.1 us
    unnamed x269, local copies, waits for them, and re-layouts  41.3 us
    dot_general x9, matrix products, mm_tn(): lax.dot_general(a, b, (((0,), (0,)), ((), ())), preferred_element_type=F32)  38.9 us
    dot_general x10, matrix products, mm(): return jnp.dot(a, b, preferred_element_type=F32)  38.9 us
    dot_general x9, matrix products, mm_nt(): lax.dot_general(a, b, (((1,), (1,)), ((), ())), preferred_element_type=F32)  33.5 us
  transfers between devices with their start and end apart: 9, of which 6 were waited for; matrix products, arithmetic and copies ran while one was open for 27% of the time, Pallas kernels for 0%

profile of v1, /device:TPU:0, one launch (start us, length us, event | category | flops | bytes accessed | tf_op | source)
XLA Modules:
  0.0 831.6 jit_solution(6843104572083162282)
XLA Ops:
  12.7 43.1 %all_to_all.42 = bf16[4,256,768]{2,1,0:T(8,128)(2,1)S(1)} all-to-all(bf16[4,256,768]{2,1,0:T(8,128)(2,1)S(1)} %copy-done.34), channel_id=1, replica_groups=mesh['fsdp'=8,'sp'=4] {'sp'}, dimensions={0} | all-to-all | bytes 3145728 | tf_op jit(solution)/shard_map/all_to_all | solution.py:231
  67.4 28.0 %all-to-all-done.2 = bf16[4,256,768]{2,1,0:T(8,128)(2,1)S(1)} async-done(((bf16[4,256,768]{2,1,0:T(8,128)(2,1)}), bf16[4,256,768]{2,1,0:T(8,128)(2,1)S(1)}, u32[]{:S(2)}, u32[]{:S(2)}) %all-to-all-start.2) | async-done | bytes 1572896 | tf_op jit(solution)/shard_map/all_to_all | solution.py:231
  135.9 11.2 %fusion.132 = (f32[12,256]{1,0:T(8,128)}, f32[12,256,1024]{2,1,0:T(8,128)}) fusion(pred[256,1024]{1,0:T(8,128)(4,1)} %get-tuple-element.80, bf16[256,12,64]{0,2,1:T(8,128)(2,1)} %bitcast.338, bf16[1024,12,64]{0,2,1:T(8,128)(2,1)} %bitcast.259), kind=kOutput, calls=%fused_computation.236 | convolution fusion | flops 412091392 | bytes 14823424 | tf_op jit(solution)/shard_map/sub | solution.py:88
  147.1 10.7 %fusion.133 = (f32[12,256]{1,0:T(8,128)}, f32[12,256,1024]{2,1,0:T(8,128)}) fusion(pred[256,1024]{1,0:T(8,128)(4,1)} %get-tuple-element.79, bf16[256,12,64]{0,2,1:T(8,128)(2,1)} %bitcast.315, bf16[1024,12,64]{0,2,1:T(8,128)(2,1)} %bitcast.260), kind=kOutput, calls=%fused_computation.237 | convolution fusion | flops 412091392 | bytes 14823424 | tf_op jit(solution)/shard_map/sub | solution.py:88
  157.8 10.8 %fusion.134 = (f32[12,256]{1,0:T(8,128)}, f32[12,256,1024]{2,1,0:T(8,128)}) fusion(pred[256,1024]{1,0:T(8,128)(4,1)} %get-tuple-element.78, bf16[256,12,64]{0,2,1:T(8,128)(2,1)} %bitcast.313, bf16[1024,12,64]{0,2,1:T(8,128)(2,1)} %bitcast.261), kind=kOutput, calls=%fused_computation.238 | convolution fusion | flops 412091392 | bytes 14823424 | tf_op jit(solution)/shard_map/sub | solution.py:88
  168.7 10.8 %fusion.135 = (f32[12,256]{1,0:T(8,128)}, f32[12,256,1024]{2,1,0:T(8,128)}) fusion(pred[256,1024]{1,0:T(8,128)(4,1)} %get-tuple-element.77, bf16[256,12,64]{0,2,1:T(8,128)(2,1)S(1)} %bitcast.311, bf16[1024,12,64]{0,2,1:T(8,128)(2,1)} %bitcast.262), kind=kOutput, calls=%fused_computation.239 | convolution fusion | flops 412091392 | bytes 14823424 | tf_op jit(solution)/shard_map/sub | solution.py:88
  217.1 14.3 %multiply_convert_fusion.4 = (bf16[1024,3072]{1,0:T(8,128)(2,1)}, f32[1024,3072]{1,0:T(8,128)}) fusion(f32[3072]{0:T(1024)S(1)} %copy-done.84, bf16[768,768]{1,0:T(8,128)(2,1)} %bitcast.355, bf16[768,768]{1,0:T(8,128)(2,1)} %bitcast.357, bf16[768,768]{1,0:T(8,128)(2,1)} %bitcast.359, bf16[768,768]{1,0:T(8,128)(2,1)} %bitcast.353, ...), kind=kOutput, calls=%fused_computation.20 | convolution fusion | flops 4873519104 | bytes 26765312 | tf_op jit(solution)/shard_map/dot_general | solution.py:31
  231.4 7.7 fusion.138
  244.4 15.3 %fusion.140 = (bf16[3072]{0:T(1024)(128)(2,1)}, bf16[1024,3072]{1,0:T(8,128)(2,1)}) fusion(f32[1024,3072]{1,0:T(8,128)} %get-tuple-element.94, f32[3072]{0:T(1024)S(1)} %copy-done.84, bf16[3072,768]{1,0:T(8,128)(2,1)S(1)} %bitcast.308, f32[1024,768]{0,1:T(8,128)S(1)} %get-tuple-element.50), kind=kOutput, calls=%fused_computation.244 | convolution fusion | flops 4870370304 | bytes 26757120 | tf_op jit(solution)/shard_map/dot_general | solution.py:35
  259.8 9.4 %multiply_reduce_fusion.5 = (bf16[768]{0:T(1024)(128)(2,1)}, f32[1024]{0:T(1024)S(1)}, f32[1024]{0:T(1024)S(1)}, bf16[768]{0:T(1024)(128)(2,1)}, f32[1024,768]{0,1:T(8,128)S(1)}) fusion(f32[1024,768]{0,1:T(8,128)S(1)} %copy-done.14, f32[1024]{0:T(1024)S(1)} %add_rsqrt_fusion.1, f32[1024]{0:T(1024)S(1)} %broadcast_multiply_fusion.4, f32[768]{0:T(1024)S(1)} %mul.222, ...), kind=kOutput, calls=%fused_computation.57 | convolution fusion | flops 4858572800 | bytes 20469760 | tf_op jit(solution)/shard_map/dot_general | solution.py:35
  282.9 8.0 fusion.41
  290.9 8.2 fusion.37
  302.3 8.2 multiply_reduce_fusion
  348.8 7.7 multiply_reduce_fusion.3
  443.4 10.5 %convolution_convert_fusion.1 = bf16[768,3072]{1,0:T(8,128)(2,1)} fusion(bf16[1024,3072]{1,0:T(8,128)(2,1)} %get-tuple-element.115, f32[1024,768]{0,1:T(8,128)S(1)} %copy-done.15, f32[768]{0:T(1024)S(1)} %copy-done.94, f32[768]{0:T(1024)S(1)} %copy-done.71, f32[1024]{0:T(1024)S(1)} %copy-done.73, f32[1024]{0:T(1024)S(1)} %copy-done.66), kind=kOutput, calls=%fused_computation.49 | convolution fusion | flops 4838129664 | bytes 14170112 | tf_op jit(solution)/shard_map/dot_general | solution.py:39
  453.9 10.0 %convert_element_type.326 = bf16[768,4,768]{2,1,0:T(4,128)(2,1)} reshape(bf16[768,3072]{1,0:T(8,128)(2,1)} %convolution_convert_fusion.1) | data formatting | bytes 9437184 | tf_op jit(solution)/shard_map/convert_element_type | solution.py:297
  468.0 8.6 %convolution_convert_fusion = bf16[3072,768]{1,0:T(8,128)(2,1)S(1)} fusion(bf16[1024,3072]{1,0:T(8,128)(2,1)} %get-tuple-element.93, f32[1024,768]{0,1:T(8,128)S(1)} %copy-done.21), kind=kOutput, calls=%fused_computation.48 | convolution fusion | flops 4834983936 | bytes 14155776 | tf_op jit(solution)/shard_map/dot_general | solution.py:39
  480.7 31.5 %reduce-scatter.3.cloned.1.call-done = bf16[1,674,768]{2,1,0:T(8,128)(2,1)} async-done(((bf16[8,674,768]{2,1,0:T(8,128)(2,1)}), bf16[1,674,768]{2,1,0:T(8,128)(2,1)}) %reduce-scatter.3.cloned.1.call-update) | async-done | bytes 1035280 | tf_op jit(solution)/shard_map/reduce_scatter | solution.py:326
  512.2 80.2 %reduce-scatter.5.cloned.1.call-done = bf16[1,768,768]{2,1,0:T(8,128)(2,1)} async-done(((bf16[8,768,768]{2,1,0:T(8,128)(2,1)}), bf16[1,768,768]{2,1,0:T(8,128)(2,1)}) %reduce-scatter.5.cloned.1.call-update) | async-done | bytes 1179664 | tf_op jit(solution)/shard_map/reduce_scatter | solution.py:326
  600.4 11.8 %reduce.67 = bf16[1024,768]{1,0:T(8,128)(2,1)} reduce(bf16[1024,1,768]{2,1,0:T(2,128)(2,1)S(1)} %bitcast.297, bf16[]{:T(256)} %broadcast.289), dimensions={1}, to_apply=%bitcast.157.reduce_sub_computation | reduce | bytes 3145730
  641.3 11.8 %reduce.68 = bf16[1024,768]{1,0:T(8,128)(2,1)} reduce(bf16[1024,1,768]{2,1,0:T(2,128)(2,1)S(1)} %bitcast.298, bf16[]{:T(256)} %broadcast.289), dimensions={1}, to_apply=%bitcast.159.reduce_sub_computation | reduce | bytes 3145730
  656.8 42.8 %all-to-all-done.1 = bf16[4,2,98304]{2,1,0:T(2,128)(2,1)} async-done(((bf16[4,2,98304]{2,1,0:T(2,128)(2,1)}), bf16[4,2,98304]{2,1,0:T(2,128)(2,1)}, u32[]{:S(2)}, u32[]{:S(2)}) %all-to-all-start.1) | async-done | bytes 1572896 | tf_op jit(solution)/shard_map/all_to_all | solution.py:234
  708.7 69.0 %all-to-all-done.3 = bf16[4,2,98304]{2,1,0:T(2,128)(2,1)} async-done(((bf16[4,2,98304]{2,1,0:T(2,128)(2,1)}), bf16[4,2,98304]{2,1,0:T(2,128)(2,1)}, u32[]{:S(2)}, u32[]{:S(2)}) %all-to-all-start.3) | async-done | bytes 1572896 | tf_op jit(solution)/shard_map/all_to_all | solution.py:234
  789.6 28.6 %all-gather.10.cloned.1.call-done = bf16[4,768,768]{2,1,0:T(8,128)(2,1)} async-done(((bf16[1,768,768]{2,1,0:T(8,128)(2,1)}), bf16[4,768,768]{2,1,0:T(8,128)(2,1)}) %all-gather.10.cloned.1.call-update) | async-done | bytes 4718608 | tf_op jit(solution)/shard_map/all_gather | solution.py:327
  (452 shorter events, 317.5 us)
Async XLA Ops:
  7.2 55.6 %copy-start = (s32[4,4]{1,0:T(4,128)S(1)}, s32[4,4]{1,0:T(4,128)}, u32[]{:S(2)}) copy-start(s32[4,4]{1,0:T(4,128)} %param.13) | copy-start | bytes 196
  7.2 91.1 %all-gather.14.cloned.1.call-start = ((), (), s32[]{:S(2)}) async-start(), calls=%async_computation.11 | async-start | bytes 9400320 | tf_op jit(solution)/shard_map/all_gather | solution.py:250
  55.8 39.7 %all-to-all-start.2 = ((bf16[4,256,768]{2,1,0:T(8,128)(2,1)}), bf16[4,256,768]{2,1,0:T(8,128)(2,1)S(1)}, u32[]{:S(2)}, u32[]{:S(2)}) async-start(bf16[4,256,768]{2,1,0:T(8,128)(2,1)} %param.23), calls=%async_computation.2 | async-start | bytes 3145728 | tf_op jit(solution)/shard_map/all_to_all | solution.py:231
  59.4 147.3 %all-gather.12.cloned.1.call-start = ((), (), s32[]{:S(2)}) async-start(), calls=%async_computation.10 | async-start | bytes 10616832 | tf_op jit(solution)/shard_map/all_gather | solution.py:251
  62.7 449.4 %reduce-scatter.3.cloned.1.call-start = ((), (), s32[]{:S(2)}) async-start(), calls=%async_computation.6 | async-start | bytes 9400320 | tf_op jit(solution)/shard_map/reduce_scatter | solution.py:326
  62.8 33.0 %copy-start.85 = (s32[4]{0:T(128)}, s32[4]{0:T(128)S(1)}, u32[]{:S(2)}) copy-start(s32[4]{0:T(128)S(1)} %dynamic-slice_bitcast_fusion) | copy-start | bytes 52
  101.0 168.2 %copy-start.70 = (f32[768]{0:T(1024)}, f32[768]{0:T(1024)S(1)}, u32[]{:S(2)}) copy-start(f32[768]{0:T(1024)S(1)} %mul.222) | copy-start | bytes 9220
  129.3 39.3 %copy-start.22 = (bf16[256,768]{0,1:T(8,128)(2,1)}, bf16[256,768]{0,1:T(8,128)(2,1)S(1)}, u32[]{:S(2)}) copy-start(bf16[256,768]{0,1:T(8,128)(2,1)S(1)} %get-tuple-element.65) | copy-start | bytes 1179652
  204.5 64.7 %copy-start.65 = (f32[1024]{0:T(1024)}, f32[1024]{0:T(1024)S(1)}, u32[]{:S(2)}) copy-start(f32[1024]{0:T(1024)S(1)} %broadcast_multiply_fusion.4) | copy-start | bytes 12292
  206.6 62.6 %copy-start.72 = (f32[1024]{0:T(1024)}, f32[1024]{0:T(1024)S(1)}, u32[]{:S(2)}) copy-start(f32[1024]{0:T(1024)S(1)} %add_rsqrt_fusion.1) | copy-start | bytes 12292
  244.4 15.3 %copy-start.52 = (bf16[8,96,768]{2,1,0:T(8,128)(2,1)S(1)}, bf16[8,96,768]{2,1,0:T(8,128)(2,1)}, u32[]{:S(2)}) copy-start(bf16[8,96,768]{2,1,0:T(8,128)(2,1)} %get-tuple-element.53) | copy-start | bytes 3538948
  244.4 15.3 %copy-start.53 = (bf16[8,96,768]{2,1,0:T(8,128)(2,1)S(1)}, bf16[8,96,768]{2,1,0:T(8,128)(2,1)}, u32[]{:S(2)}) copy-start(bf16[8,96,768]{2,1,0:T(8,128)(2,1)} %get-tuple-element.54) | copy-start | bytes 3538948
  244.4 15.3 %copy-start.54 = (bf16[8,96,768]{2,1,0:T(8,128)(2,1)S(1)}, bf16[8,96,768]{2,1,0:T(8,128)(2,1)}, u32[]{:S(2)}) copy-start(bf16[8,96,768]{2,1,0:T(8,128)(2,1)} %get-tuple-element.55) | copy-start | bytes 3538948
  244.4 15.3 %copy-start.55 = (bf16[8,96,768]{2,1,0:T(8,128)(2,1)S(1)}, bf16[8,96,768]{2,1,0:T(8,128)(2,1)}, u32[]{:S(2)}) copy-start(bf16[8,96,768]{2,1,0:T(8,128)(2,1)} %get-tuple-element.56) | copy-start | bytes 3538948
  276.0 34.6 %copy-start.38 = (bf16[1024,12,64]{0,2,1:T(8,128)(2,1)}, bf16[1024,12,64]{0,2,1:T(8,128)(2,1)S(1)}, u32[]{:S(2)}) copy-start(bf16[1024,12,64]{0,2,1:T(8,128)(2,1)S(1)} %multiply_convert_fusion.5) | copy-start | bytes 4718596
  282.8 16.2 %slice-start.9 = ((s8[12582912]{0:T(1024)(128)(4,1)}), s8[4194304]{0:T(1024)(128)(4,1)S(1)}, s32[]{:S(2)}) async-start(s8[12582912]{0:T(1024)(128)(4,1)} %bitcast.289), calls=%async_computation.21 | async-start | bytes 8388608
  282.8 16.2 %slice-start.10 = ((s8[12582912]{0:T(1024)(128)(4,1)}), s8[4194304]{0:T(1024)(128)(4,1)S(1)}, s32[]{:S(2)}) async-start(s8[12582912]{0:T(1024)(128)(4,1)} %bitcast.289), calls=%async_computation.22 | async-start | bytes 8388608
  344.8 33.3 %copy-start.26 = (bf16[12,64,256]{2,1,0:T(8,128)(2,1)}, bf16[12,64,256]{2,1,0:T(8,128)(2,1)S(1)}, u32[]{:S(2)}) copy-start(bf16[12,64,256]{2,1,0:T(8,128)(2,1)S(1)} %convolution_convert_fusion.16) | copy-start | bytes 1179652
  441.6 150.8 %reduce-scatter.5.cloned.1.call-start = ((), (), s32[]{:S(2)}) async-start(), calls=%async_computation.8 | async-start | bytes 10616832 | tf_op jit(solution)/shard_map/reduce_scatter | solution.py:326
  480.6 111.8 %copy-start.61 = (bf16[4,12,64]{2,1,0:T(8,128)(2,1)S(1)}, bf16[4,12,64]{2,1,0:T(8,128)(2,1)}, u32[]{:S(2)}) copy-start(bf16[4,12,64]{2,1,0:T(8,128)(2,1)} %copy.106) | copy-start | bytes 18436
  480.6 301.5 %all-gather.8.cloned.1.call-start = ((), (), s32[]{:S(2)}) async-start(), calls=%async_computation.7 | async-start | bytes 5222400 | tf_op jit(solution)/shard_map/all_gather | solution.py:327
  512.2 306.0 %all-gather.10.cloned.1.call-start = ((), (), s32[]{:S(2)}) async-start(), calls=%async_computation.9 | async-start | bytes 5898240 | tf_op jit(solution)/shard_map/all_gather | solution.py:327
  616.1 83.5 %all-to-all-start.1 = ((bf16[4,2,98304]{2,1,0:T(2,128)(2,1)}), bf16[4,2,98304]{2,1,0:T(2,128)(2,1)}, u32[]{:S(2)}, u32[]{:S(2)}) async-start(bf16[4,2,98304]{2,1,0:T(2,128)(2,1)} %reshape.661), calls=%async_computation.1 | async-start | bytes 3145728 | tf_op jit(solution)/shard_map/all_to_all | solution.py:234
  699.6 78.1 %all-to-all-start.3 = ((bf16[4,2,98304]{2,1,0:T(2,128)(2,1)}), bf16[4,2,98304]{2,1,0:T(2,128)(2,1)}, u32[]{:S(2)}, u32[]{:S(2)}) async-start(bf16[4,2,98304]{2,1,0:T(2,128)(2,1)} %reshape.663), calls=%async_computation.3 | async-start | bytes 3145728 | tf_op jit(solution)/shard_map/all_to_all | solution.py:234
  (112 other events, 499.5 us)
Sparse Core Ops, SparseCore 0:
  12.8 56.9 all-gather.13
  72.3 58.8 all-gather.11
  441.7 70.3 reduce-scatter.2
  515.9 76.4 reduce-scatter.4
  593.9 113.8 all-gather.7
  709.3 108.8 all-gather.9
